TPU v7x, 32 devices: a whole 2x2x4 slice. The times are simulated.
32 devices in a mesh: group: 8 (over y, x, core), rep: 4 (over z).
Axes of the slice: x: 2, y: 2, z: 4, core: 2. Of those that a mesh axis runs over, the one named last changes fastest.
Arguments:
- tokens: bfloat16 [8192, 768], P(('group', 'rep')), may hold values from -6 to 6
- segments: int32 [8192], P(('group', 'rep')), may hold values from -1 to 3, as said below
- attn_in_weight: bfloat16 [2, 768, 2304], P(None, 'group'), may hold values from -8 to 8
- attn_bias: bfloat16 [2, 3, 768], P(None, None, 'group'), may hold values from -1.75 to 1.75
- out_weight: bfloat16 [2, 768, 768], P(None, 'group'), may hold values from -0.875 to 0.875
- fc1_weight: bfloat16 [2, 768, 3072], P(None, 'group'), may hold values from -0.21875 to 0.21875
- fc1_bias: bfloat16 [2, 3072], P(None, 'group'), may hold values from -1.75 to 1.75
- fc2_weight: bfloat16 [2, 3072, 768], P(None, 'group'), may hold values from -0.109375 to 0.109375
- fc2_bias: bfloat16 [2, 768], P(None, 'group'), may hold values from -1.75 to 1.75
- ln_gain: bfloat16 [2, 2, 768], P(None, None, 'group'), may hold values from 0.25 to 1.75
- ln_bias: bfloat16 [2, 2, 768], P(None, None, 'group'), may hold values from -1.75 to 1.75
- cotangent: bfloat16 [8192, 768], P(('group', 'rep')), may hold values from -12 to 12
Outputs:
- output: float32 [8192, 768], P(('group', 'rep'))
- input_grad: float32 [8192, 768], P(('group', 'rep'))
- grad_attn_in: float32 [2, 768, 2304], P(None, 'group')
- grad_attn_bias: float32 [2, 3, 768], P(None, None, 'group')
- grad_out_weight: float32 [2, 768, 768], P(None, 'group')
- grad_fc1_weight: float32 [2, 768, 3072], P(None, 'group')
- grad_fc1_bias: float32 [2, 3072], P(None, 'group')
- grad_fc2_weight: float32 [2, 3072, 768], P(None, 'group')
- grad_fc2_bias: float32 [2, 768], P(None, 'group')
- grad_ln_gain: float32 [2, 2, 768], P(None, None, 'group')
- grad_ln_bias: float32 [2, 2, 768], P(None, None, 'group')
Inputs may be any that keep to these rules, and one draw needn't show every extreme that they name: `segments`: each clip occupies exactly 1500 consecutive positions, clip numbers rise by one along the tokens, the first clip starts at the first token, padding elsewhere.
All inputs are finite; a program needn't handle non-finite values.
Results may differ from a plain program's by a relative error of at most 0.017.
Values may be sent and summed in bfloat16 or wider, within the bound.
No kernel may reach another device: no remote copies, remote signals or barrier semaphores. Data moves between devices by JAX's collectives and lax.ppermute only.
A program may use at most 256 MiB of HBM per device.

v0:
```python
import jax
import jax.numpy as jnp
from jax import lax
from jax.sharding import PartitionSpec as P

H = 12
HD = 64
LAYERS = 2
REACH = 6
EPSILON = 1e-05


def passed_along(value, axis, steps):
    count = lax.axis_size(axis)
    leading, last = (max(0, -steps), min(count, count - steps))
    return lax.ppermute(value, axis, [(source, source + steps) for source in range(leading, last)])


def layer_norm(values, gain, offset):
    center = jnp.mean(values, axis=-1, keepdims=True)
    shifted = values - center
    spread = jnp.mean(shifted * shifted, axis=-1, keepdims=True)
    inverse = lax.rsqrt(spread + EPSILON)
    unit_rows = shifted * inverse
    return (unit_rows * gain.astype(jnp.float32) + offset.astype(jnp.float32), unit_rows, inverse)


def norm_back(upstream, unit_rows, inverse, gain):
    scaled = upstream * gain.astype(jnp.float32)
    result = inverse * (
        scaled
        - jnp.mean(scaled, axis=-1, keepdims=True)
        - unit_rows * jnp.mean(scaled * unit_rows, axis=-1, keepdims=True)
    )
    return (result, jnp.sum(upstream * unit_rows, axis=0), jnp.sum(upstream, axis=0))


def gelu_slope(inputs):
    normal_cdf = 0.5 * (1.0 + lax.erf(inputs * 0.7071067811865476))
    return normal_cdf + inputs * jnp.exp(-0.5 * inputs * inputs) * 0.3989422804014327


def split_heads(matrix):
    return matrix.reshape(matrix.shape[0], H // 2, 2, HD).transpose(1, 0, 2, 3)


def join_heads(stacked):
    return stacked.transpose(1, 0, 2, 3).reshape(stacked.shape[1], H * HD)


def head_forward(queries, key_block, value_block, allowed):
    scores = jnp.einsum("qhd,khd->hqk", queries, key_block, preferred_element_type=jnp.float32)
    scores = jnp.where(allowed[None], scores, -1e30)
    top_score = jnp.max(scores, axis=2, keepdims=True)
    expd = jnp.exp(scores - top_score)
    total = jnp.sum(expd, axis=2, keepdims=True)
    probs = (expd / total).astype(jnp.bfloat16)
    heard = jnp.einsum("hqk,khd->qhd", probs, value_block, preferred_element_type=jnp.float32)
    return (heard, top_score[:, :, 0] + jnp.log(total[:, :, 0]))


def head_backward(queries, key_block, value_block, allowed, log_totals, upstream):
    scores = jnp.einsum("qhd,khd->hqk", queries, key_block, preferred_element_type=jnp.float32)
    probs = jnp.where(allowed[None], jnp.exp(scores - log_totals[:, :, None]), 0.0)
    rounded = probs.astype(jnp.bfloat16)
    d_value = jnp.einsum("hqk,qhd->khd", rounded, upstream, preferred_element_type=jnp.float32)
    d_probs = jnp.einsum("qhd,khd->hqk", upstream, value_block, preferred_element_type=jnp.float32)
    delta = jnp.sum(probs * d_probs, axis=2, keepdims=True)
    d_scores = (probs * (d_probs - delta)).astype(jnp.bfloat16)
    d_query = jnp.einsum("hqk,khd->qhd", d_scores, key_block, preferred_element_type=jnp.float32)
    d_key = jnp.einsum("hqk,qhd->khd", d_scores, queries, preferred_element_type=jnp.float32)
    return (d_query, d_key, d_value)


def local(
    tokens,
    segments,
    attn_in_weight,
    attn_bias,
    out_weight,
    fc1_weight,
    fc1_bias,
    fc2_weight,
    fc2_bias,
    ln_gain,
    ln_bias,
    cotangent,
):
    tok_rows = tokens.shape[0]
    width = H * HD
    score_scale = HD ** (-0.5)
    labels = segments + 2
    own_place = lax.iota(jnp.int32, tok_rows) + REACH * tok_rows
    window_place = lax.iota(jnp.int32, (2 * REACH + 1) * tok_rows)
    resid = tokens.astype(jnp.float32)
    fetched = []
    every_store = []
    for layer_at in range(LAYERS):
        weights = (
            lax.all_gather(attn_in_weight[layer_at], "group", axis=0, tiled=True),
            lax.all_gather(attn_bias[layer_at], "group", axis=1, tiled=True),
            lax.all_gather(out_weight[layer_at], "group", axis=0, tiled=True),
            lax.all_gather(fc1_weight[layer_at], "group", axis=0, tiled=True),
            lax.all_gather(fc1_bias[layer_at], "group", axis=0, tiled=True),
            lax.all_gather(fc2_weight[layer_at], "group", axis=0, tiled=True),
            lax.all_gather(fc2_bias[layer_at], "group", axis=0, tiled=True),
            lax.all_gather(ln_gain[layer_at], "group", axis=1, tiled=True),
            lax.all_gather(ln_bias[layer_at], "group", axis=1, tiled=True),
        )
        (
            forward_w_in,
            forward_b_attn,
            forward_w_out,
            forward_w_up,
            forward_b_up,
            forward_w_down,
            forward_b_down,
            forward_gains,
            forward_offsets,
        ) = weights
        normed, forward_unit_first, forward_inverse_first = layer_norm(
            resid, forward_gains[0], forward_offsets[0]
        )
        forward_first = normed.astype(jnp.bfloat16)
        mixed = jnp.dot(forward_first, forward_w_in, preferred_element_type=jnp.float32)
        forward_queries = (
            (mixed[:, :width] + forward_b_attn[0].astype(jnp.float32)) * score_scale
        ).astype(jnp.bfloat16)
        forward_key_value = jnp.concatenate(
            [
                mixed[:, width : 2 * width],
                mixed[:, 2 * width :] + forward_b_attn[1].astype(jnp.float32),
            ],
            axis=1,
        ).astype(jnp.bfloat16)
        lower_parts = []
        upper_parts = []
        for gather_distance in range(1, REACH + 1):
            lower_parts.append(
                passed_along((forward_key_value, labels), ("group", "rep"), gather_distance)
            )
            upper_parts.append(
                passed_along((forward_key_value, labels), ("group", "rep"), -gather_distance)
            )
        ordered = lower_parts[::-1] + [(forward_key_value, labels)] + upper_parts
        window_rows = jnp.concatenate([member[0] for member in ordered], axis=0)
        window_labels = jnp.concatenate([member[1] for member in ordered], axis=0)
        same = labels[:, None] == window_labels[None, :]
        forward_allowed = same & (
            (labels[:, None] >= 2) | (own_place[:, None] == window_place[None, :])
        )

        def attend_pair(members):
            return head_forward(members[0], members[1], members[2], forward_allowed)

        attended, forward_log_totals = lax.map(
            attend_pair,
            (
                split_heads(forward_queries),
                split_heads(window_rows[:, :width]),
                split_heads(window_rows[:, width:]),
            ),
        )
        forward_heard = join_heads(attended).astype(jnp.bfloat16)
        middle = (
            resid
            + jnp.dot(forward_heard, forward_w_out, preferred_element_type=jnp.float32)
            + forward_b_attn[2].astype(jnp.float32)
        )
        normed_two, forward_unit_second, forward_inverse_second = layer_norm(
            middle, forward_gains[1], forward_offsets[1]
        )
        forward_second = normed_two.astype(jnp.bfloat16)
        forward_pre_act = jnp.dot(
            forward_second, forward_w_up, preferred_element_type=jnp.float32
        ) + forward_b_up.astype(jnp.float32)
        forward_active = jax.nn.gelu(forward_pre_act, approximate=False).astype(jnp.bfloat16)
        result = (
            middle
            + jnp.dot(forward_active, forward_w_down, preferred_element_type=jnp.float32)
            + forward_b_down.astype(jnp.float32)
        )
        forward_stored = (
            forward_unit_first,
            forward_inverse_first,
            forward_first,
            forward_queries,
            window_rows,
            forward_allowed,
            forward_heard,
            forward_log_totals,
            forward_unit_second,
            forward_inverse_second,
            forward_second,
            forward_pre_act,
            forward_active,
        )
        resid = result
        fetched.append(None)
        every_store.append(forward_stored)
    upstream = cotangent.astype(jnp.float32)
    shares = [None] * LAYERS
    for layer_at in reversed(range(LAYERS)):
        weights = (
            lax.all_gather(attn_in_weight[layer_at], "group", axis=0, tiled=True),
            lax.all_gather(attn_bias[layer_at], "group", axis=1, tiled=True),
            lax.all_gather(out_weight[layer_at], "group", axis=0, tiled=True),
            lax.all_gather(fc1_weight[layer_at], "group", axis=0, tiled=True),
            lax.all_gather(fc1_bias[layer_at], "group", axis=0, tiled=True),
            lax.all_gather(fc2_weight[layer_at], "group", axis=0, tiled=True),
            lax.all_gather(fc2_bias[layer_at], "group", axis=0, tiled=True),
            lax.all_gather(ln_gain[layer_at], "group", axis=1, tiled=True),
            lax.all_gather(ln_bias[layer_at], "group", axis=1, tiled=True),
        )
        w_in, b_attn, w_out, w_up, b_up, w_down, b_down, gains, offsets = weights
        (
            unit_first,
            inverse_first,
            first,
            queries,
            window_kv,
            allowed,
            heard,
            log_totals,
            unit_second,
            inverse_second,
            second,
            pre_act,
            active,
        ) = every_store[layer_at]
        down_rounded = upstream.astype(jnp.bfloat16)
        g_down_b = jnp.sum(upstream, axis=0)
        g_down_w = jnp.einsum("tf,td->fd", active, down_rounded, preferred_element_type=jnp.float32)
        d_pre = jnp.einsum(
            "td,fd->tf", down_rounded, w_down, preferred_element_type=jnp.float32
        ) * gelu_slope(pre_act)
        up_rounded = d_pre.astype(jnp.bfloat16)
        g_up_b = jnp.sum(d_pre, axis=0)
        g_up_w = jnp.einsum("td,tf->df", second, up_rounded, preferred_element_type=jnp.float32)
        d_second = jnp.einsum("tf,df->td", up_rounded, w_up, preferred_element_type=jnp.float32)
        d_norm_two, g_gain_two, g_offset_two = norm_back(
            d_second, unit_second, inverse_second, gains[1]
        )
        d_middle = upstream + d_norm_two
        middle_rounded = d_middle.astype(jnp.bfloat16)
        g_out_b = jnp.sum(d_middle, axis=0)
        g_out_w = jnp.einsum("td,te->de", heard, middle_rounded, preferred_element_type=jnp.float32)
        d_heard = jnp.einsum(
            "te,de->td", middle_rounded, w_out, preferred_element_type=jnp.float32
        ).astype(jnp.bfloat16)

        def pair_backward(members):
            return head_backward(
                members[0], members[1], members[2], allowed, members[3], members[4]
            )

        d_query, d_key, d_value = lax.map(
            pair_backward,
            (
                split_heads(queries),
                split_heads(window_kv[:, :width]),
                split_heads(window_kv[:, width:]),
                log_totals,
                split_heads(d_heard),
            ),
        )
        d_window = jnp.concatenate([join_heads(d_key), join_heads(d_value)], axis=1)
        d_own = d_window[REACH * tok_rows : (REACH + 1) * tok_rows]
        for distance in range(1, REACH + 1):
            lower_block = d_window[
                (REACH - distance) * tok_rows : (REACH - distance + 1) * tok_rows
            ]
            upper_block = d_window[
                (REACH + distance) * tok_rows : (REACH + distance + 1) * tok_rows
            ]
            d_own = d_own + passed_along(
                lower_block.astype(jnp.bfloat16), ("group", "rep"), -distance
            ).astype(lower_block.dtype)
            d_own = d_own + passed_along(
                upper_block.astype(jnp.bfloat16), ("group", "rep"), distance
            ).astype(upper_block.dtype)
        d_queries = join_heads(d_query) * score_scale
        d_mixed = jnp.concatenate([d_queries, d_own], axis=1)
        mixed_rounded = d_mixed.astype(jnp.bfloat16)
        g_attn_b = jnp.stack(
            [jnp.sum(d_queries, axis=0), jnp.sum(d_own[:, width:], axis=0), g_out_b]
        )
        g_in_w = jnp.einsum("td,te->de", first, mixed_rounded, preferred_element_type=jnp.float32)
        d_first = jnp.einsum("te,de->td", mixed_rounded, w_in, preferred_element_type=jnp.float32)
        d_norm_one, g_gain_one, g_offset_one = norm_back(
            d_first, unit_first, inverse_first, gains[0]
        )
        d_resid = d_middle + d_norm_one
        grads = (
            g_in_w,
            g_attn_b,
            g_out_w,
            g_up_w,
            g_up_b,
            g_down_w,
            g_down_b,
            jnp.stack([g_gain_one, g_gain_two]),
            jnp.stack([g_offset_one, g_offset_two]),
        )
        upstream, grads = (d_resid, grads)
        summed = (
            lax.psum_scatter(
                grads[0].astype(jnp.bfloat16), "group", scatter_dimension=0, tiled=True
            ).astype(jnp.float32),
            lax.psum_scatter(
                grads[1].astype(jnp.bfloat16), "group", scatter_dimension=1, tiled=True
            ).astype(jnp.float32),
            lax.psum_scatter(
                grads[2].astype(jnp.bfloat16), "group", scatter_dimension=0, tiled=True
            ).astype(jnp.float32),
            lax.psum_scatter(
                grads[3].astype(jnp.bfloat16), "group", scatter_dimension=0, tiled=True
            ).astype(jnp.float32),
            lax.psum_scatter(
                grads[4].astype(jnp.bfloat16), "group", scatter_dimension=0, tiled=True
            ).astype(jnp.float32),
            lax.psum_scatter(
                grads[5].astype(jnp.bfloat16), "group", scatter_dimension=0, tiled=True
            ).astype(jnp.float32),
            lax.psum_scatter(
                grads[6].astype(jnp.bfloat16), "group", scatter_dimension=0, tiled=True
            ).astype(jnp.float32),
            lax.psum_scatter(
                grads[7].astype(jnp.bfloat16), "group", scatter_dimension=1, tiled=True
            ).astype(jnp.float32),
            lax.psum_scatter(
                grads[8].astype(jnp.bfloat16), "group", scatter_dimension=1, tiled=True
            ).astype(jnp.float32),
        )
        summed = (
            lax.psum(summed[0].astype(jnp.bfloat16), "rep").astype(jnp.float32),
            lax.psum(summed[1].astype(jnp.bfloat16), "rep").astype(jnp.float32),
            lax.psum(summed[2].astype(jnp.bfloat16), "rep").astype(jnp.float32),
            lax.psum(summed[3].astype(jnp.bfloat16), "rep").astype(jnp.float32),
            lax.psum(summed[4].astype(jnp.bfloat16), "rep").astype(jnp.float32),
            lax.psum(summed[5].astype(jnp.bfloat16), "rep").astype(jnp.float32),
            lax.psum(summed[6].astype(jnp.bfloat16), "rep").astype(jnp.float32),
            lax.psum(summed[7].astype(jnp.bfloat16), "rep").astype(jnp.float32),
            lax.psum(summed[8].astype(jnp.bfloat16), "rep").astype(jnp.float32),
        )
        shares[layer_at] = summed
    stacked = [
        jnp.stack([shares[layer_at][field] for layer_at in range(LAYERS)]) for field in range(9)
    ]
    return (
        resid,
        upstream,
        stacked[0],
        stacked[1],
        stacked[2],
        stacked[3],
        stacked[4],
        stacked[5],
        stacked[6],
        stacked[7],
        stacked[8],
    )


def solution(mesh):
    in_specs = (
        P(("group", "rep"), None),
        P(("group", "rep")),
        P(None, "group", None),
        P(None, None, "group"),
        P(None, "group", None),
        P(None, "group", None),
        P(None, "group"),
        P(None, "group", None),
        P(None, "group"),
        P(None, None, "group"),
        P(None, None, "group"),
        P(("group", "rep"), None),
    )
    out_specs = (
        P(("group", "rep"), None),
        P(("group", "rep"), None),
        P(None, "group", None),
        P(None, None, "group"),
        P(None, "group", None),
        P(None, "group", None),
        P(None, "group"),
        P(None, "group", None),
        P(None, "group"),
        P(None, None, "group"),
        P(None, None, "group"),
    )
    return jax.shard_map(local, mesh=mesh, in_specs=in_specs, out_specs=out_specs, check_vma=False)
```

profile of v0, /device:TPU:0, one launch (start us, length us, event | category | flops | bytes accessed | tf_op | source)
XLA Modules:
  0.0 2316.4 jit_solution(14734667101272722325)
XLA Ops:
  198.8 30.9 %collective-permute-done.23 = s32[256]{0:T(256)S(1)} collective-permute-done((s32[256]{0:T(256)S(1)}, s32[256]{0:T(256)S(1)}, u32[]{:S(2)}, u32[]{:S(2)}) %collective-permute-start.23) | collective-permute-done | bytes 1056 | tf_op jit(solution)/shard_map/ppermute | solution.py:16
  238.5 32.8 %collective-permute-start.5 = (bf16[256,1536]{1,0:T(8,128)(2,1)S(1)}, bf16[256,1536]{1,0:T(8,128)(2,1)S(1)}, u32[]{:S(2)}, u32[]{:S(2)}) collective-permute-start(bf16[256,1536]{1,0:T(8,128)(2,1)S(1)} %pad_maximum_fusion.4), channel_id=1, source_target_pairs={{0,1},{1,2},{2,3},{3,4},{4,5},{5,6},{6,7},{7,8},{8,9},{9,10},{10,1... | collective-permute-start | bytes 2359304 | tf_op jit(solution)/shard_map/ppermute | solution.py:16
  292.3 18.6 collective-permute-done.6
  313.2 66.3 %collective-permute-done.7 = bf16[256,1536]{1,0:T(8,128)(2,1)S(1)} collective-permute-done((bf16[256,1536]{1,0:T(8,128)(2,1)S(1)}, bf16[256,1536]{1,0:T(8,128)(2,1)S(1)}, u32[]{:S(2)}, u32[]{:S(2)}) %collective-permute-start.7) | collective-permute-done | bytes 786464 | tf_op jit(solution)/shard_map/ppermute | solution.py:16
  421.0 46.2 %while.56 = (s32[]{:T(128)}, bf16[6,256,2,64]{1,3,2,0:T(8,128)(2,1)S(1)}, f32[6,2,256]{2,1,0:T(2,128)S(1)}, bf16[6,3328,2,64]{1,3,2,0:T(8,128)(2,1)}, bf16[6,256...) while((s32[]{:T(128)}, ...), condition=%wide.region_5.6_spmd.clone, body=%wide.region_2.5_spmd.clone.sunk | while | flops 451542528 | bytes 24085872 | solution.py:156
  489.2 17.5 collective-permute-start.24
  529.0 50.0 %all-gather.15 = bf16[1,3072]{1,0:T(2,128)(2,1)S(1)} all-gather(bf16[1,384]{1,0:T(2,128)(2,1)S(1)} %get-tuple-element.563), channel_id=17, replica_groups=mesh['group'=8,'rep'=4] {'group'}, dimensions={1}, use_global_device_ids=true | all-gather | bytes 6912 | tf_op jit(solution)/shard_map/all_gather | solution.py:104
  628.8 84.9 %collective-permute-done.31 = bf16[256,1536]{1,0:T(8,128)(2,1)S(1)} collective-permute-done((bf16[256,1536]{1,0:T(8,128)(2,1)S(1)}, bf16[256,1536]{1,0:T(8,128)(2,1)S(1)}, u32[]{:S(2)}, u32[]{:S(2)}) %collective-permute-start.31) | collective-permute-done | bytes 786464 | tf_op jit(solution)/shard_map/ppermute | solution.py:16
  752.4 46.2 %while.57 = (s32[]{:T(128)}, bf16[6,256,2,64]{1,3,2,0:T(8,128)(2,1)S(1)}, f32[6,2,256]{2,1,0:T(2,128)S(1)}, bf16[6,3328,2,64]{1,3,2,0:T(8,128)(2,1)}, bf16[6,256...) while((s32[]{:T(128)}, ...), condition=%wide.region_13.14_spmd.clone, body=%wide.region_10.13_spmd.clone.sunk | while | flops 451542528 | bytes 24085872 | solution.py:156
  833.7 121.5 %while.58 = (s32[]{:T(128)}, f32[6,256,2,64]{1,3,2,0:T(8,128)}, f32[6,3328,2,64]{1,3,2,0:T(8,128)}, f32[6,3328,2,64]{1,3,2,0:T(8,128)}, bf16[6,3328,2,64]{1,3,2,...) while((s32[]{:T(128)}, f32[6,256,2,64]{1,3,2,0:T(8,128)}, ...), condition=%wide.region_20.21_spmd.clone, body=%wide.region_18.20_spmd.clone.sunk | while | flops 1107557888 | bytes 75987424 | solution.py:257
  974.7 27.5 %collective-permute-start.39 = (bf16[256,1536]{0,1:T(8,128)(2,1)S(1)}, bf16[256,1536]{0,1:T(8,128)(2,1)S(1)}, u32[]{:S(2)}, u32[]{:S(2)}) collective-permute-start(bf16[256,1536]{0,1:T(8,128)(2,1)S(1)} %get-tuple-element.538), channel_id=1, source_target_pairs={{0,2},{1,3},{2,4},{3,5},{4,6},{5,7},{6,8},{7,9},{8,10},{9,11},{10,... | collective-permute-start | bytes 2359304 | tf_op jit(solution)/shard_map/ppermute | solution.py:16
  1017.0 66.7 %collective-permute-done.38 = bf16[256,1536]{0,1:T(8,128)(2,1)S(1)} collective-permute-done((bf16[256,1536]{0,1:T(8,128)(2,1)S(1)}, bf16[256,1536]{0,1:T(8,128)(2,1)S(1)}, u32[]{:S(2)}, u32[]{:S(2)}) %collective-permute-start.38) | collective-permute-done | bytes 786464 | tf_op jit(solution)/shard_map/ppermute | solution.py:16
  1100.7 48.4 %collective-permute-start.47 = (bf16[256,1536]{0,1:T(8,128)(2,1)S(1)}, bf16[256,1536]{0,1:T(8,128)(2,1)}, u32[]{:S(2)}, u32[]{:S(2)}) collective-permute-start(bf16[256,1536]{0,1:T(8,128)(2,1)S(1)} %get-tuple-element.530), channel_id=1, source_target_pairs={{0,6},{1,7},{2,8},{3,9},{4,10},{5,11},{6,12},{7,13},{8,14},{9,15},... | collective-permute-start | bytes 2359304 | tf_op jit(solution)/shard_map/ppermute | solution.py:16
  1152.7 35.9 %collective-permute-done.46 = bf16[256,1536]{0,1:T(8,128)(2,1)} collective-permute-done((bf16[256,1536]{0,1:T(8,128)(2,1)}, bf16[256,1536]{0,1:T(8,128)(2,1)}, u32[]{:S(2)}, u32[]{:S(2)}) %collective-permute-start.46) | collective-permute-done | bytes 786464 | tf_op jit(solution)/shard_map/ppermute | solution.py:16
  1219.3 126.5 %while.59 = (s32[]{:T(128)}, f32[6,256,2,64]{1,3,2,0:T(8,128)}, f32[6,3328,2,64]{1,3,2,0:T(8,128)}, f32[6,3328,2,64]{1,3,2,0:T(8,128)}, bf16[6,3328,2,64]{1,3,2,...) while((s32[]{:T(128)}, f32[6,256,2,64]{1,3,2,0:T(8,128)}, ...), condition=%wide.region_27.28_spmd.clone, body=%wide.region_25.27_spmd.clone.sunk | while | flops 1107557888 | bytes 75987424 | solution.py:257
  1350.3 16.8 fusion.90
  1382.8 23.1 collective-permute-start.51
  1420.8 66.4 %collective-permute-done.50 = bf16[256,1536]{0,1:T(8,128)(2,1)S(1)} collective-permute-done((bf16[256,1536]{0,1:T(8,128)(2,1)S(1)}, bf16[256,1536]{0,1:T(8,128)(2,1)S(1)}, u32[]{:S(2)}, u32[]{:S(2)}) %collective-permute-start.50) | collective-permute-done | bytes 786464 | tf_op jit(solution)/shard_map/ppermute | solution.py:16
  1512.4 49.2 %collective-permute-start.59 = (bf16[256,1536]{0,1:T(8,128)(2,1)S(1)}, bf16[256,1536]{0,1:T(8,128)(2,1)S(1)}, u32[]{:S(2)}, u32[]{:S(2)}) collective-permute-start(bf16[256,1536]{0,1:T(8,128)(2,1)S(1)} %get-tuple-element.518), channel_id=1, source_target_pairs={{0,6},{1,7},{2,8},{3,9},{4,10},{5,11},{6,12},{7,13},{8,14},{9,15},... | collective-permute-start | bytes 2359304 | tf_op jit(solution)/shard_map/ppermute | solution.py:16
  1563.0 20.7 collective-permute-done.58
  1630.0 85.8 %reduce-scatter.27.cloned.1.call-done = bf16[96,2304]{1,0:T(8,128)(2,1)} async-done(((bf16[768,2304]{1,0:T(8,128)(2,1)}), bf16[96,2304]{1,0:T(8,128)(2,1)}) %reduce-scatter.27.cloned.1.call-update) | async-done | bytes 442384 | tf_op jit(solution)/shard_map/reduce_scatter | solution.py:307
  1715.8 57.2 %reduce-scatter.37.cloned.1.call-done = bf16[96,3072]{1,0:T(8,128)(2,1)} async-done(((bf16[768,3072]{1,0:T(8,128)(2,1)}), bf16[96,3072]{1,0:T(8,128)(2,1)}) %reduce-scatter.37.cloned.1.call-update) | async-done | bytes 589840 | tf_op jit(solution)/shard_map/reduce_scatter | solution.py:316
  1773.0 57.1 %reduce-scatter.41.cloned.1.call-done = bf16[384,768]{1,0:T(8,128)(2,1)} async-done(((bf16[3072,768]{1,0:T(8,128)(2,1)}), bf16[384,768]{1,0:T(8,128)(2,1)}) %reduce-scatter.41.cloned.1.call-update) | async-done | bytes 589840 | tf_op jit(solution)/shard_map/reduce_scatter | solution.py:322
  1830.2 57.1 %reduce-scatter.39.cloned.1.call-done = bf16[384,768]{1,0:T(8,128)(2,1)} async-done(((bf16[3072,768]{1,0:T(8,128)(2,1)}), bf16[384,768]{1,0:T(8,128)(2,1)}) %reduce-scatter.39.cloned.1.call-update) | async-done | bytes 589840 | tf_op jit(solution)/shard_map/reduce_scatter | solution.py:322
  1887.3 57.1 %reduce-scatter.35.cloned.1.call-done = bf16[96,3072]{1,0:T(8,128)(2,1)} async-done(((bf16[768,3072]{1,0:T(8,128)(2,1)}), bf16[96,3072]{1,0:T(8,128)(2,1)}) %reduce-scatter.35.cloned.1.call-update) | async-done | bytes 589840 | tf_op jit(solution)/shard_map/reduce_scatter | solution.py:316
  1946.0 22.9 all-reduce.6
  1981.8 36.3 %reduce-scatter.49.cloned.1.call-done = bf16[96,2]{1,0:T(8,128)(2,1)} async-done(((bf16[768,2]{1,0:T(8,128)(2,1)}), bf16[96,2]{1,0:T(8,128)(2,1)}) %reduce-scatter.49.cloned.1.call-update) | async-done | bytes 400
  2018.9 36.5 %reduce-scatter.45.cloned.1.call-done = bf16[96,3]{1,0:T(8,128)(2,1)} async-done(((bf16[768,3]{1,0:T(8,128)(2,1)}), bf16[96,3]{1,0:T(8,128)(2,1)}) %reduce-scatter.45.cloned.1.call-update) | async-done | bytes 592
  2057.4 34.5 %reduce-scatter.51.cloned.1.call-done = bf16[96,2]{1,0:T(8,128)(2,1)} async-done(((bf16[768,2]{1,0:T(8,128)(2,1)}), bf16[96,2]{1,0:T(8,128)(2,1)}) %reduce-scatter.51.cloned.1.call-update) | async-done | bytes 400
  2092.7 35.9 %reduce-scatter.47.cloned.1.call-done = bf16[96,2]{1,0:T(8,128)(2,1)} async-done(((bf16[768,2]{1,0:T(8,128)(2,1)}), bf16[96,2]{1,0:T(8,128)(2,1)}) %reduce-scatter.47.cloned.1.call-update) | async-done | bytes 400
  2129.5 36.5 %reduce-scatter.43.cloned.1.call-done = bf16[96,3]{1,0:T(8,128)(2,1)} async-done(((bf16[768,3]{1,0:T(8,128)(2,1)}), bf16[96,3]{1,0:T(8,128)(2,1)}) %reduce-scatter.43.cloned.1.call-update) | async-done | bytes 592
  2181.6 121.3 %all-reduce.11.cloned.1.call-done = (bf16[1,96,2304]{2,1,0:T(8,128)(2,1)}, bf16[1,96,2304]{2,1,0:T(8,128)(2,1)}, bf16[1,96,768]{2,1,0:T(8,128)(2,1)}, bf16[1,96,...) async-done(((bf16[1,96,2304]{2,1,0:T(8,128)(2,1)}, ...) | async-done | bytes 3538960 | tf_op jit(solution)/shard_map/psum | solution.py:336
  (833 shorter events, 1002.9 us)
Async XLA Ops:
  7.2 155.8 %all-gather.27.cloned.1.call-start = ((), (), s32[]{:S(2)}) async-start(), calls=%async_computation.22 | async-start | bytes 3981312 | tf_op jit(solution)/shard_map/all_gather | solution.py:100
  9.5 457.7 %all-gather.29.cloned.1.call-start = ((), (), s32[]{:S(2)}) async-start(), calls=%async_computation.23 | async-start | bytes 1327104 | tf_op jit(solution)/shard_map/all_gather | solution.py:102
  11.3 458.3 %all-gather.31.cloned.1.call-start = ((), (), s32[]{:S(2)}) async-start(), calls=%async_computation.24 | async-start | bytes 5308416 | tf_op jit(solution)/shard_map/all_gather | solution.py:103
  12.5 468.6 %all-gather.33.cloned.1.call-start = ((), (), s32[]{:S(2)}) async-start(), calls=%async_computation.25 | async-start | bytes 5308416 | tf_op jit(solution)/shard_map/all_gather | solution.py:105
  13.7 472.0 %all-gather.35.cloned.1.call-start = ((), (), s32[]{:S(2)}) async-start(), calls=%async_computation.26 | async-start | bytes 3981312 | tf_op jit(solution)/shard_map/all_gather | solution.py:100
  14.3 784.3 %all-gather.37.cloned.1.call-start = ((), (), s32[]{:S(2)}) async-start(), calls=%async_computation.27 | async-start | bytes 1327104 | tf_op jit(solution)/shard_map/all_gather | solution.py:102
  14.9 785.9 %all-gather.39.cloned.1.call-start = ((), (), s32[]{:S(2)}) async-start(), calls=%async_computation.28 | async-start | bytes 5308416 | tf_op jit(solution)/shard_map/all_gather | solution.py:103
  14.9 139.6 %collective-permute-start.12 = (s32[256]{0:T(256)S(1)}, s32[256]{0:T(256)S(1)}, u32[]{:S(2)}, u32[]{:S(2)}) collective-permute-start(s32[256]{0:T(256)S(1)} %broadcast_add_fusion), channel_id=1, source_target_pairs={{0,6},{1,7},{2,8},{3,9},{4,10},{5,11},{6,12},{7,13},{8,14},{9,15},... | collective-permute-start | bytes 3080 | tf_op jit(solution)/shard_map/ppermute | solution.py:16
  20.4 137.1 %collective-permute-start.13 = (s32[256]{0:T(256)S(1)}, s32[256]{0:T(256)S(1)}, u32[]{:S(2)}, u32[]{:S(2)}) collective-permute-start(s32[256]{0:T(256)S(1)} %broadcast_add_fusion), channel_id=1, source_target_pairs={{0,5},{1,6},{2,7},{3,8},{4,9},{5,10},{6,11},{7,12},{8,13},{9,14},{... | collective-permute-start | bytes 3080 | tf_op jit(solution)/shard_map/ppermute | solution.py:16
  25.0 133.7 %collective-permute-start.14 = (s32[256]{0:T(256)S(1)}, s32[256]{0:T(256)S(1)}, u32[]{:S(2)}, u32[]{:S(2)}) collective-permute-start(s32[256]{0:T(256)S(1)} %broadcast_add_fusion), channel_id=1, source_target_pairs={{0,4},{1,5},{2,6},{3,7},{4,8},{5,9},{6,10},{7,11},{8,12},{9,13},{1... | collective-permute-start | bytes 3080 | tf_op jit(solution)/shard_map/ppermute | solution.py:16
  26.8 133.3 %collective-permute-start.15 = (s32[256]{0:T(256)S(1)}, s32[256]{0:T(256)S(1)}, u32[]{:S(2)}, u32[]{:S(2)}) collective-permute-start(s32[256]{0:T(256)S(1)} %broadcast_add_fusion), channel_id=1, source_target_pairs={{0,3},{1,4},{2,5},{3,6},{4,7},{5,8},{6,9},{7,10},{8,11},{9,12},{10... | collective-permute-start | bytes 3080 | tf_op jit(solution)/shard_map/ppermute | solution.py:16
  32.2 129.3 %collective-permute-start.16 = (s32[256]{0:T(256)S(1)}, s32[256]{0:T(256)S(1)}, u32[]{:S(2)}, u32[]{:S(2)}) collective-permute-start(s32[256]{0:T(256)S(1)} %broadcast_add_fusion), channel_id=1, source_target_pairs={{0,2},{1,3},{2,4},{3,5},{4,6},{5,7},{6,8},{7,9},{8,10},{9,11},{10,... | collective-permute-start | bytes 3080 | tf_op jit(solution)/shard_map/ppermute | solution.py:16
  33.5 778.4 %all-gather.41.cloned.1.call-start = ((), (), s32[]{:S(2)}) async-start(), calls=%async_computation.29 | async-start | bytes 5308416 | tf_op jit(solution)/shard_map/all_gather | solution.py:105
  529.0 1101.0 %reduce-scatter.33.cloned.1.call-start = ((), (), s32[]{:S(2)}) async-start(), calls=%async_computation.17 | async-start | bytes 1327104 | tf_op jit(solution)/shard_map/reduce_scatter | solution.py:313
  588.2 125.5 %collective-permute-start.31 = (bf16[256,1536]{1,0:T(8,128)(2,1)S(1)}, bf16[256,1536]{1,0:T(8,128)(2,1)S(1)}, u32[]{:S(2)}, u32[]{:S(2)}) collective-permute-start(bf16[256,1536]{1,0:T(8,128)(2,1)S(1)} %pad_maximum_fusion.5), channel_id=1, source_target_pairs={{2,0},{3,1},{4,2},{5,3},{6,4},{7,5},{8,6},{9,7},{10,8},{11,9},{12,... | collective-permute-start | bytes 2359304 | tf_op jit(solution)/shard_map/ppermute | solution.py:16
  591.6 123.0 %collective-permute-start.32 = (bf16[256,1536]{1,0:T(8,128)(2,1)S(1)}, bf16[256,1536]{1,0:T(8,128)(2,1)S(1)}, u32[]{:S(2)}, u32[]{:S(2)}) collective-permute-start(bf16[256,1536]{1,0:T(8,128)(2,1)S(1)} %pad_maximum_fusion.5), channel_id=1, source_target_pairs={{3,0},{4,1},{5,2},{6,3},{7,4},{8,5},{9,6},{10,7},{11,8},{12,9},{13... | collective-permute-start | bytes 2359304 | tf_op jit(solution)/shard_map/ppermute | solution.py:16
  598.2 117.4 %collective-permute-start.33 = (bf16[256,1536]{1,0:T(8,128)(2,1)S(1)}, bf16[256,1536]{1,0:T(8,128)(2,1)S(1)}, u32[]{:S(2)}, u32[]{:S(2)}) collective-permute-start(bf16[256,1536]{1,0:T(8,128)(2,1)S(1)} %pad_maximum_fusion.5), channel_id=1, source_target_pairs={{4,0},{5,1},{6,2},{7,3},{8,4},{9,5},{10,6},{11,7},{12,8},{13,9},{1... | collective-permute-start | bytes 2359304 | tf_op jit(solution)/shard_map/ppermute | solution.py:16
  974.7 116.4 %collective-permute-start.39 = (bf16[256,1536]{0,1:T(8,128)(2,1)S(1)}, bf16[256,1536]{0,1:T(8,128)(2,1)S(1)}, u32[]{:S(2)}, u32[]{:S(2)}) collective-permute-start(bf16[256,1536]{0,1:T(8,128)(2,1)S(1)} %get-tuple-element.538), channel_id=1, source_target_pairs={{0,2},{1,3},{2,4},{3,5},{4,6},{5,7},{6,8},{7,9},{8,10},{9,11},{10,... | collective-permute-start | bytes 2359304 | tf_op jit(solution)/shard_map/ppermute | solution.py:16
  1150.7 479.3 %reduce-scatter.31.cloned.1.call-start = ((), (), s32[]{:S(2)}) async-start(), calls=%async_computation.16 | async-start | bytes 1327104 | tf_op jit(solution)/shard_map/reduce_scatter | solution.py:313
  1208.7 421.3 %reduce-scatter.29.cloned.1.call-start = ((), (), s32[]{:S(2)}) async-start(), calls=%async_computation.15 | async-start | bytes 3981312 | tf_op jit(solution)/shard_map/reduce_scatter | solution.py:307
  1350.2 365.6 %reduce-scatter.27.cloned.1.call-start = ((), (), s32[]{:S(2)}) async-start(), calls=%async_computation.14 | async-start | bytes 3981312 | tf_op jit(solution)/shard_map/reduce_scatter | solution.py:307
  1593.7 179.3 %reduce-scatter.37.cloned.1.call-start = ((), (), s32[]{:S(2)}) async-start(), calls=%async_computation.19 | async-start | bytes 5308416 | tf_op jit(solution)/shard_map/reduce_scatter | solution.py:316
  1600.1 230.1 %reduce-scatter.41.cloned.1.call-start = ((), (), s32[]{:S(2)}) async-start(), calls=%async_computation.21 | async-start | bytes 5308416 | tf_op jit(solution)/shard_map/reduce_scatter | solution.py:322
  1606.1 281.2 %reduce-scatter.39.cloned.1.call-start = ((), (), s32[]{:S(2)}) async-start(), calls=%async_computation.20 | async-start | bytes 5308416 | tf_op jit(solution)/shard_map/reduce_scatter | solution.py:322
  1611.5 332.9 %reduce-scatter.35.cloned.1.call-start = ((), (), s32[]{:S(2)}) async-start(), calls=%async_computation.18 | async-start | bytes 5308416 | tf_op jit(solution)/shard_map/reduce_scatter | solution.py:316
  1617.3 363.7 %reduce-scatter.53.cloned.1.call-start = ((), (), s32[]{:S(2)}) async-start(), calls=%async_computation.35 | async-start | bytes 221184
  1620.3 397.8 %reduce-scatter.49.cloned.1.call-start = ((), (), s32[]{:S(2)}) async-start(), calls=%async_computation.33 | async-start | bytes 221184
  1621.2 434.2 %reduce-scatter.45.cloned.1.call-start = ((), (), s32[]{:S(2)}) async-start(), calls=%async_computation.31 | async-start | bytes 221184
  1622.3 469.7 %reduce-scatter.51.cloned.1.call-start = ((), (), s32[]{:S(2)}) async-start(), calls=%async_computation.34 | async-start | bytes 221184
  1627.8 500.9 %reduce-scatter.47.cloned.1.call-start = ((), (), s32[]{:S(2)}) async-start(), calls=%async_computation.32 | async-start | bytes 221184
  1628.7 537.2 %reduce-scatter.43.cloned.1.call-start = ((), (), s32[]{:S(2)}) async-start(), calls=%async_computation.30 | async-start | bytes 221184
  1629.7 673.2 %all-reduce.11.cloned.1.call-start = ((), (), s32[]{:S(2)}) async-start(), calls=%async_computation.36 | async-start | bytes 7077888 | tf_op jit(solution)/shard_map/psum | solution.py:336
  (199 other events, 10318.9 us)
Sparse Core Ops, SparseCore 0:
  10.5 38.1 all-gather.26
  50.5 24.4 all-gather.28
  77.5 40.9 all-gather.30
  120.8 38.9 all-gather.32
  162.1 33.7 all-gather.34
  197.6 56.4 all-gather.36
  256.6 47.6 all-gather.38
  529.1 74.4 all-gather.40
  1150.8 48.1 reduce-scatter.32
  1208.8 77.4 reduce-scatter.30
  1350.3 98.4 reduce-scatter.28
  1593.9 121.8 reduce-scatter.26
  1719.2 53.7 reduce-scatter.36
  1776.3 53.7 reduce-scatter.40
  1833.5 53.7 reduce-scatter.38
  1890.6 53.7 reduce-scatter.34
  1947.2 33.6 reduce-scatter.52
  1984.4 33.6 reduce-scatter.48
  2021.7 33.6 reduce-scatter.44
  2058.2 33.6 reduce-scatter.50
  2095.0 33.6 reduce-scatter.46
  2132.2 33.6 reduce-scatter.42
  2168.9 133.9 all-reduce.10
where the time goes:
time: 2330 us; the launch traced here: 2320 us
  waiting for transfers between devices  1060 us (45%)
  starting transfers between devices  398 us (17%)
  matrix products  349 us (15%)
  other arithmetic  174 us (7%)
  blocking collectives  168 us (7%)
  local copies, waits for them, and re-layouts  143 us (6%)
    ppermute x60, waiting for transfers between devices, passed_along(): lax.ppermute(value, axis, [(source, source + steps) for source in range(l...  440 us
    ppermute x60, starting transfers between devices, passed_along(): lax.ppermute(value, axis, [(source, source + steps) for source in range(l...  397 us
    unnamed x29, waiting for transfers between devices  188 us
    psum x1, waiting for transfers between devices, local(): lax.psum(summed[0].astype(jnp.bfloat16), 'rep').astype(jnp.float32)  121 us
    reduce_scatter x2, waiting for transfers between devices, local(): lax.psum_scatter(grads[3].astype(jnp.bfloat16), 'group', scatter_dimensio...  114 us
    reduce_scatter x2, waiting for transfers between devices, local(): lax.psum_scatter(grads[5].astype(jnp.bfloat16), 'group', scatter_dimensio...  114 us
    reduce_scatter x2, waiting for transfers between devices, local(): lax.psum_scatter(grads[0].astype(jnp.bfloat16), 'group', scatter_dimensio...  85.8 us
    all_gather x2, blocking collectives, local(): lax.all_gather(fc1_bias[layer_at], 'group', axis=0, tiled=True)  58.5 us
  transfers between devices with their start and end apart: 83, of which 26 were waited for; matrix products, arithmetic and copies ran while one was open for 21% of the time, Pallas kernels for 0%

commit v1 on v0

--- a/solution.py
+++ b/solution.py
@@ -333,7 +333,9 @@
             ).astype(jnp.float32),
         )
         summed = (
-            lax.psum(summed[0].astype(jnp.bfloat16), "rep").astype(jnp.float32),
+            jnp.sum(lax.all_gather(summed[0].astype(jnp.bfloat16), "rep"), axis=0).astype(
+                jnp.float32
+            ),
             lax.psum(summed[1].astype(jnp.bfloat16), "rep").astype(jnp.float32),
             lax.psum(summed[2].astype(jnp.bfloat16), "rep").astype(jnp.float32),
             lax.psum(summed[3].astype(jnp.bfloat16), "rep").astype(jnp.float32),

time: 2330 us -> 2470 us (1.060)
  waiting for transfers between devices: 1060 us -> 1190 us
    reduce_scatter x2, waiting for transfers between devices: 0.04 us -> 79.7 us  [local(): lax.psum_scatter(grads[2].astype(jnp.bfloat16), 'group', scatter_dimensio...]
    all_gather x0 -> x2, waiting for transfers between devices: none -> 65 us  [local(): lax.all_gather(summed[0].astype(jnp.bfloat16), 'rep')]
    unnamed x284 -> x298, local copies, waits for them, and re-layouts: 53.4 us -> 54.4 us
    unnamed x29 -> x31, waiting for transfers between devices: 188 us -> 188 us
  transfers between devices with their start and end apart: 83 -> 85, of which waited for: 26 -> 30; matrix products, arithmetic and copies ran while one was open for 21% -> 14% of each run, Pallas kernels for 0% -> 0%
where the time goes in v1:
time: 2470 us; the launch traced here: 2450 us
  waiting for transfers between devices  1190 us (48%)
  starting transfers between devices  399 us (16%)
  matrix products  346 us (14%)
  other arithmetic  182 us (7%)
  blocking collectives  168 us (7%)
  local copies, waits for them, and re-layouts  150 us (6%)
    ppermute x60, waiting for transfers between devices, passed_along(): lax.ppermute(value, axis, [(source, source + steps) for source in range(l...  441 us
    ppermute x60, starting transfers between devices, passed_along(): lax.ppermute(value, axis, [(source, source + steps) for source in range(l...  398 us
    unnamed x31, waiting for transfers between devices  188 us
    reduce_scatter x2, waiting for transfers between devices, local(): lax.psum_scatter(grads[3].astype(jnp.bfloat16), 'group', scatter_dimensio...  114 us
    reduce_scatter x2, waiting for transfers between devices, local(): lax.psum_scatter(grads[5].astype(jnp.bfloat16), 'group', scatter_dimensio...  114 us
    psum x1, waiting for transfers between devices, local(): lax.psum(summed[2].astype(jnp.bfloat16), 'rep').astype(jnp.float32)  104 us
    reduce_scatter x2, waiting for transfers between devices, local(): lax.psum_scatter(grads[2].astype(jnp.bfloat16), 'group', scatter_dimensio...  79.7 us
    reduce_scatter x2, waiting for transfers between devices, local(): lax.psum_scatter(grads[0].astype(jnp.bfloat16), 'group', scatter_dimensio...  79 us
  transfers between devices with their start and end apart: 85, of which 30 were waited for; matrix products, arithmetic and copies ran while one was open for 14% of the time, Pallas kernels for 0%

profile of v1, /device:TPU:0, one launch (start us, length us, event | category | flops | bytes accessed | tf_op | source)
XLA Modules:
  0.0 2451.6 jit_solution(17659904451931129895)
XLA Ops:
  198.9 30.8 %collective-permute-done.23 = s32[256]{0:T(256)S(1)} collective-permute-done((s32[256]{0:T(256)S(1)}, s32[256]{0:T(256)S(1)}, u32[]{:S(2)}, u32[]{:S(2)}) %collective-permute-start.23) | collective-permute-done | bytes 1056 | tf_op jit(solution)/shard_map/ppermute | solution.py:16
  238.5 32.8 %collective-permute-start.5 = (bf16[256,1536]{1,0:T(8,128)(2,1)S(1)}, bf16[256,1536]{1,0:T(8,128)(2,1)S(1)}, u32[]{:S(2)}, u32[]{:S(2)}) collective-permute-start(bf16[256,1536]{1,0:T(8,128)(2,1)S(1)} %pad_maximum_fusion.4), channel_id=1, source_target_pairs={{0,1},{1,2},{2,3},{3,4},{4,5},{5,6},{6,7},{7,8},{8,9},{9,10},{10,1... | collective-permute-start | bytes 2359304 | tf_op jit(solution)/shard_map/ppermute | solution.py:16
  313.1 66.3 %collective-permute-done.7 = bf16[256,1536]{1,0:T(8,128)(2,1)S(1)} collective-permute-done((bf16[256,1536]{1,0:T(8,128)(2,1)S(1)}, bf16[256,1536]{1,0:T(8,128)(2,1)S(1)}, u32[]{:S(2)}, u32[]{:S(2)}) %collective-permute-start.7) | collective-permute-done | bytes 786464 | tf_op jit(solution)/shard_map/ppermute | solution.py:16
  420.9 46.2 %while.56 = (s32[]{:T(128)}, bf16[6,256,2,64]{1,3,2,0:T(8,128)(2,1)S(1)}, f32[6,2,256]{2,1,0:T(2,128)S(1)}, bf16[6,3328,2,64]{1,3,2,0:T(8,128)(2,1)}, bf16[6,256...) while((s32[]{:T(128)}, ...), condition=%wide.region_5.6_spmd.clone, body=%wide.region_2.5_spmd.clone.sunk | while | flops 451542528 | bytes 24085872 | solution.py:156
  529.5 50.1 %all-gather.15 = bf16[1,3072]{1,0:T(2,128)(2,1)S(1)} all-gather(bf16[1,384]{1,0:T(2,128)(2,1)S(1)} %get-tuple-element.561), channel_id=17, replica_groups=mesh['group'=8,'rep'=4] {'group'}, dimensions={1}, use_global_device_ids=true | all-gather | bytes 6912 | tf_op jit(solution)/shard_map/all_gather | solution.py:104
  629.8 84.4 %collective-permute-done.31 = bf16[256,1536]{1,0:T(8,128)(2,1)S(1)} collective-permute-done((bf16[256,1536]{1,0:T(8,128)(2,1)S(1)}, bf16[256,1536]{1,0:T(8,128)(2,1)S(1)}, u32[]{:S(2)}, u32[]{:S(2)}) %collective-permute-start.31) | collective-permute-done | bytes 786464 | tf_op jit(solution)/shard_map/ppermute | solution.py:16
  752.9 46.2 %while.57 = (s32[]{:T(128)}, bf16[6,256,2,64]{1,3,2,0:T(8,128)(2,1)S(1)}, f32[6,2,256]{2,1,0:T(2,128)S(1)}, bf16[6,3328,2,64]{1,3,2,0:T(8,128)(2,1)}, bf16[6,256...) while((s32[]{:T(128)}, ...), condition=%wide.region_13.14_spmd.clone, body=%wide.region_10.13_spmd.clone.sunk | while | flops 451542528 | bytes 24085872 | solution.py:156
  834.6 118.1 %while.58 = (s32[]{:T(128)}, f32[6,256,2,64]{1,3,2,0:T(8,128)}, f32[6,3328,2,64]{1,3,2,0:T(8,128)}, f32[6,3328,2,64]{1,3,2,0:T(8,128)}, bf16[6,3328,2,64]{1,3,2,...) while((s32[]{:T(128)}, f32[6,256,2,64]{1,3,2,0:T(8,128)}, ...), condition=%wide.region_20.21_spmd.clone, body=%wide.region_18.20_spmd.clone.sunk | while | flops 1107557888 | bytes 72841640 | solution.py:257
  981.3 27.5 %collective-permute-start.39 = (bf16[256,1536]{0,1:T(8,128)(2,1)S(1)}, bf16[256,1536]{0,1:T(8,128)(2,1)S(1)}, u32[]{:S(2)}, u32[]{:S(2)}) collective-permute-start(bf16[256,1536]{0,1:T(8,128)(2,1)S(1)} %get-tuple-element.536), channel_id=1, source_target_pairs={{0,2},{1,3},{2,4},{3,5},{4,6},{5,7},{6,8},{7,9},{8,10},{9,11},{10,... | collective-permute-start | bytes 2359304 | tf_op jit(solution)/shard_map/ppermute | solution.py:16
  1023.6 66.7 %collective-permute-done.38 = bf16[256,1536]{0,1:T(8,128)(2,1)S(1)} collective-permute-done((bf16[256,1536]{0,1:T(8,128)(2,1)S(1)}, bf16[256,1536]{0,1:T(8,128)(2,1)S(1)}, u32[]{:S(2)}, u32[]{:S(2)}) %collective-permute-start.38) | collective-permute-done | bytes 786464 | tf_op jit(solution)/shard_map/ppermute | solution.py:16
  1106.4 48.3 %collective-permute-start.47 = (bf16[256,1536]{0,1:T(8,128)(2,1)S(1)}, bf16[256,1536]{0,1:T(8,128)(2,1)S(1)}, u32[]{:S(2)}, u32[]{:S(2)}) collective-permute-start(bf16[256,1536]{0,1:T(8,128)(2,1)S(1)} %get-tuple-element.528), channel_id=1, source_target_pairs={{0,6},{1,7},{2,8},{3,9},{4,10},{5,11},{6,12},{7,13},{8,14},{9,15},... | collective-permute-start | bytes 2359304 | tf_op jit(solution)/shard_map/ppermute | solution.py:16
  1156.7 37.8 %collective-permute-done.46 = bf16[256,1536]{0,1:T(8,128)(2,1)S(1)} collective-permute-done((bf16[256,1536]{0,1:T(8,128)(2,1)S(1)}, bf16[256,1536]{0,1:T(8,128)(2,1)S(1)}, u32[]{:S(2)}, u32[]{:S(2)}) %collective-permute-start.46) | collective-permute-done | bytes 786464 | tf_op jit(solution)/shard_map/ppermute | solution.py:16
  1228.1 126.1 %while.59 = (s32[]{:T(128)}, f32[6,256,2,64]{1,3,2,0:T(8,128)}, f32[6,3328,2,64]{1,3,2,0:T(8,128)}, f32[6,3328,2,64]{1,3,2,0:T(8,128)}, bf16[6,3328,2,64]{1,3,2,...) while((s32[]{:T(128)}, f32[6,256,2,64]{1,3,2,0:T(8,128)}, ...), condition=%wide.region_27.28_spmd.clone, body=%wide.region_25.27_spmd.clone.sunk | while | flops 1107557888 | bytes 75987424 | solution.py:257
  1387.0 22.9 collective-permute-start.51
  1425.2 65.7 %collective-permute-done.50 = bf16[256,1536]{0,1:T(8,128)(2,1)S(1)} collective-permute-done((bf16[256,1536]{0,1:T(8,128)(2,1)S(1)}, bf16[256,1536]{0,1:T(8,128)(2,1)S(1)}, u32[]{:S(2)}, u32[]{:S(2)}) %collective-permute-start.50) | collective-permute-done | bytes 786464 | tf_op jit(solution)/shard_map/ppermute | solution.py:16
  1517.0 49.1 %collective-permute-start.59 = (bf16[256,1536]{0,1:T(8,128)(2,1)S(1)}, bf16[256,1536]{0,1:T(8,128)(2,1)S(1)}, u32[]{:S(2)}, u32[]{:S(2)}) collective-permute-start(bf16[256,1536]{0,1:T(8,128)(2,1)S(1)} %get-tuple-element.516), channel_id=1, source_target_pairs={{0,6},{1,7},{2,8},{3,9},{4,10},{5,11},{6,12},{7,13},{8,14},{9,15},... | collective-permute-start | bytes 2359304 | tf_op jit(solution)/shard_map/ppermute | solution.py:16
  1641.3 78.9 %reduce-scatter.27.cloned.1.call-done = bf16[96,2304]{1,0:T(8,128)(2,1)} async-done(((bf16[768,2304]{1,0:T(8,128)(2,1)}), bf16[96,2304]{1,0:T(8,128)(2,1)}) %reduce-scatter.27.cloned.1.call-update) | async-done | bytes 442384 | tf_op jit(solution)/shard_map/reduce_scatter | solution.py:307
  1720.3 39.9 %reduce-scatter.33.cloned.1.call-done = bf16[96,768]{1,0:T(8,128)(2,1)} async-done(((bf16[768,768]{1,0:T(8,128)(2,1)}), bf16[96,768]{1,0:T(8,128)(2,1)}) %reduce-scatter.33.cloned.1.call-update) | async-done | bytes 147472 | tf_op jit(solution)/shard_map/reduce_scatter | solution.py:313
  1760.2 39.8 %reduce-scatter.31.cloned.1.call-done = bf16[96,768]{1,0:T(8,128)(2,1)} async-done(((bf16[768,768]{1,0:T(8,128)(2,1)}), bf16[96,768]{1,0:T(8,128)(2,1)}) %reduce-scatter.31.cloned.1.call-update) | async-done | bytes 147472 | tf_op jit(solution)/shard_map/reduce_scatter | solution.py:313
  1800.0 57.2 %reduce-scatter.37.cloned.1.call-done = bf16[96,3072]{1,0:T(8,128)(2,1)} async-done(((bf16[768,3072]{1,0:T(8,128)(2,1)}), bf16[96,3072]{1,0:T(8,128)(2,1)}) %reduce-scatter.37.cloned.1.call-update) | async-done | bytes 589840 | tf_op jit(solution)/shard_map/reduce_scatter | solution.py:316
  1857.2 57.1 %reduce-scatter.41.cloned.1.call-done = bf16[384,768]{1,0:T(8,128)(2,1)} async-done(((bf16[3072,768]{1,0:T(8,128)(2,1)}), bf16[384,768]{1,0:T(8,128)(2,1)}) %reduce-scatter.41.cloned.1.call-update) | async-done | bytes 589840 | tf_op jit(solution)/shard_map/reduce_scatter | solution.py:322
  1914.3 57.1 %reduce-scatter.39.cloned.1.call-done = bf16[384,768]{1,0:T(8,128)(2,1)} async-done(((bf16[3072,768]{1,0:T(8,128)(2,1)}), bf16[384,768]{1,0:T(8,128)(2,1)}) %reduce-scatter.39.cloned.1.call-update) | async-done | bytes 589840 | tf_op jit(solution)/shard_map/reduce_scatter | solution.py:322
  1971.4 57.1 %reduce-scatter.35.cloned.1.call-done = bf16[96,3072]{1,0:T(8,128)(2,1)} async-done(((bf16[768,3072]{1,0:T(8,128)(2,1)}), bf16[96,3072]{1,0:T(8,128)(2,1)}) %reduce-scatter.35.cloned.1.call-update) | async-done | bytes 589840 | tf_op jit(solution)/shard_map/reduce_scatter | solution.py:316
  2030.3 22.9 all-reduce.6
  2065.9 36.3 %reduce-scatter.49.cloned.1.call-done = bf16[96,2]{1,0:T(8,128)(2,1)} async-done(((bf16[768,2]{1,0:T(8,128)(2,1)}), bf16[96,2]{1,0:T(8,128)(2,1)}) %reduce-scatter.49.cloned.1.call-update) | async-done | bytes 400
  2103.1 36.5 %reduce-scatter.45.cloned.1.call-done = bf16[96,3]{1,0:T(8,128)(2,1)} async-done(((bf16[768,3]{1,0:T(8,128)(2,1)}), bf16[96,3]{1,0:T(8,128)(2,1)}) %reduce-scatter.45.cloned.1.call-update) | async-done | bytes 592
  2141.6 34.5 %reduce-scatter.51.cloned.1.call-done = bf16[96,2]{1,0:T(8,128)(2,1)} async-done(((bf16[768,2]{1,0:T(8,128)(2,1)}), bf16[96,2]{1,0:T(8,128)(2,1)}) %reduce-scatter.51.cloned.1.call-update) | async-done | bytes 400
  2176.9 35.9 %reduce-scatter.47.cloned.1.call-done = bf16[96,2]{1,0:T(8,128)(2,1)} async-done(((bf16[768,2]{1,0:T(8,128)(2,1)}), bf16[96,2]{1,0:T(8,128)(2,1)}) %reduce-scatter.47.cloned.1.call-update) | async-done | bytes 400
  2213.6 36.4 %reduce-scatter.43.cloned.1.call-done = bf16[96,3]{1,0:T(8,128)(2,1)} async-done(((bf16[768,3]{1,0:T(8,128)(2,1)}), bf16[96,3]{1,0:T(8,128)(2,1)}) %reduce-scatter.43.cloned.1.call-update) | async-done | bytes 592
  2265.7 26.2 %all-gather.49.cloned.1.call-done = bf16[384,2304]{1,0:T(8,128)(2,1)} async-done(((bf16[96,2304]{1,0:T(8,128)(2,1)}), bf16[384,2304]{1,0:T(8,128)(2,1)}) %all-gather.49.cloned.1.call-update) | async-done | bytes 1769488 | tf_op jit(solution)/shard_map/all_gather | solution.py:336
  2293.7 38.8 %all-gather.47.cloned.1.call-done = bf16[384,2304]{1,0:T(8,128)(2,1)} async-done(((bf16[96,2304]{1,0:T(8,128)(2,1)}), bf16[384,2304]{1,0:T(8,128)(2,1)}) %all-gather.47.cloned.1.call-update) | async-done | bytes 1769488 | tf_op jit(solution)/shard_map/all_gather | solution.py:336
  2335.6 103.9 %all-reduce.11.cloned.1.call-done = (bf16[1,96,768]{2,1,0:T(8,128)(2,1)}, bf16[1,96,768]{2,1,0:T(8,128)(2,1)}, bf16[1,96,3072]{2,1,0:T(8,128)(2,1)}, bf16[1,96,3...) async-done(((bf16[1,96,768]{2,1,0:T(8,128)(2,1)}, bf16[1,96,768]{2,1,0:T(8,128)(2,1)}, bf16[1,96,3072]{2,1,0:T(8,128)(2,1)}, ...) | async-done | bytes 2654224 | tf_op jit(solution)/shard_map/psum | solution.py:340
  (832 shorter events, 1090.4 us)
Async XLA Ops:
  7.2 155.8 %all-gather.31.cloned.1.call-start = ((), (), s32[]{:S(2)}) async-start(), calls=%async_computation.22 | async-start | bytes 3981312 | tf_op jit(solution)/shard_map/all_gather | solution.py:100
  9.5 457.6 %all-gather.33.cloned.1.call-start = ((), (), s32[]{:S(2)}) async-start(), calls=%async_computation.23 | async-start | bytes 1327104 | tf_op jit(solution)/shard_map/all_gather | solution.py:102
  11.3 458.2 %all-gather.35.cloned.1.call-start = ((), (), s32[]{:S(2)}) async-start(), calls=%async_computation.24 | async-start | bytes 5308416 | tf_op jit(solution)/shard_map/all_gather | solution.py:103
  12.5 468.5 %all-gather.37.cloned.1.call-start = ((), (), s32[]{:S(2)}) async-start(), calls=%async_computation.25 | async-start | bytes 5308416 | tf_op jit(solution)/shard_map/all_gather | solution.py:105
  13.7 472.0 %all-gather.39.cloned.1.call-start = ((), (), s32[]{:S(2)}) async-start(), calls=%async_computation.26 | async-start | bytes 3981312 | tf_op jit(solution)/shard_map/all_gather | solution.py:100
  14.3 784.8 %all-gather.41.cloned.1.call-start = ((), (), s32[]{:S(2)}) async-start(), calls=%async_computation.27 | async-start | bytes 1327104 | tf_op jit(solution)/shard_map/all_gather | solution.py:102
  14.9 786.5 %all-gather.43.cloned.1.call-start = ((), (), s32[]{:S(2)}) async-start(), calls=%async_computation.28 | async-start | bytes 5308416 | tf_op jit(solution)/shard_map/all_gather | solution.py:103
  14.9 139.6 %collective-permute-start.12 = (s32[256]{0:T(256)S(1)}, s32[256]{0:T(256)S(1)}, u32[]{:S(2)}, u32[]{:S(2)}) collective-permute-start(s32[256]{0:T(256)S(1)} %broadcast_add_fusion), channel_id=1, source_target_pairs={{0,6},{1,7},{2,8},{3,9},{4,10},{5,11},{6,12},{7,13},{8,14},{9,15},... | collective-permute-start | bytes 3080 | tf_op jit(solution)/shard_map/ppermute | solution.py:16
  20.4 137.1 %collective-permute-start.13 = (s32[256]{0:T(256)S(1)}, s32[256]{0:T(256)S(1)}, u32[]{:S(2)}, u32[]{:S(2)}) collective-permute-start(s32[256]{0:T(256)S(1)} %broadcast_add_fusion), channel_id=1, source_target_pairs={{0,5},{1,6},{2,7},{3,8},{4,9},{5,10},{6,11},{7,12},{8,13},{9,14},{... | collective-permute-start | bytes 3080 | tf_op jit(solution)/shard_map/ppermute | solution.py:16
  25.1 133.7 %collective-permute-start.14 = (s32[256]{0:T(256)S(1)}, s32[256]{0:T(256)S(1)}, u32[]{:S(2)}, u32[]{:S(2)}) collective-permute-start(s32[256]{0:T(256)S(1)} %broadcast_add_fusion), channel_id=1, source_target_pairs={{0,4},{1,5},{2,6},{3,7},{4,8},{5,9},{6,10},{7,11},{8,12},{9,13},{1... | collective-permute-start | bytes 3080 | tf_op jit(solution)/shard_map/ppermute | solution.py:16
  26.8 133.3 %collective-permute-start.15 = (s32[256]{0:T(256)S(1)}, s32[256]{0:T(256)S(1)}, u32[]{:S(2)}, u32[]{:S(2)}) collective-permute-start(s32[256]{0:T(256)S(1)} %broadcast_add_fusion), channel_id=1, source_target_pairs={{0,3},{1,4},{2,5},{3,6},{4,7},{5,8},{6,9},{7,10},{8,11},{9,12},{10... | collective-permute-start | bytes 3080 | tf_op jit(solution)/shard_map/ppermute | solution.py:16
  32.2 129.3 %collective-permute-start.16 = (s32[256]{0:T(256)S(1)}, s32[256]{0:T(256)S(1)}, u32[]{:S(2)}, u32[]{:S(2)}) collective-permute-start(s32[256]{0:T(256)S(1)} %broadcast_add_fusion), channel_id=1, source_target_pairs={{0,2},{1,3},{2,4},{3,5},{4,6},{5,7},{6,8},{7,9},{8,10},{9,11},{10,... | collective-permute-start | bytes 3080 | tf_op jit(solution)/shard_map/ppermute | solution.py:16
  33.5 779.0 %all-gather.45.cloned.1.call-start = ((), (), s32[]{:S(2)}) async-start(), calls=%async_computation.29 | async-start | bytes 5308416 | tf_op jit(solution)/shard_map/all_gather | solution.py:105
  529.4 1111.1 %reduce-scatter.29.cloned.1.call-start = ((), (), s32[]{:S(2)}) async-start(), calls=%async_computation.15 | async-start | bytes 3981312 | tf_op jit(solution)/shard_map/reduce_scatter | solution.py:307
  588.7 125.5 %collective-permute-start.31 = (bf16[256,1536]{1,0:T(8,128)(2,1)S(1)}, bf16[256,1536]{1,0:T(8,128)(2,1)S(1)}, u32[]{:S(2)}, u32[]{:S(2)}) collective-permute-start(bf16[256,1536]{1,0:T(8,128)(2,1)S(1)} %pad_maximum_fusion.5), channel_id=1, source_target_pairs={{2,0},{3,1},{4,2},{5,3},{6,4},{7,5},{8,6},{9,7},{10,8},{11,9},{12,... | collective-permute-start | bytes 2359304 | tf_op jit(solution)/shard_map/ppermute | solution.py:16
  592.1 123.2 %collective-permute-start.32 = (bf16[256,1536]{1,0:T(8,128)(2,1)S(1)}, bf16[256,1536]{1,0:T(8,128)(2,1)S(1)}, u32[]{:S(2)}, u32[]{:S(2)}) collective-permute-start(bf16[256,1536]{1,0:T(8,128)(2,1)S(1)} %pad_maximum_fusion.5), channel_id=1, source_target_pairs={{3,0},{4,1},{5,2},{6,3},{7,4},{8,5},{9,6},{10,7},{11,8},{12,9},{13... | collective-permute-start | bytes 2359304 | tf_op jit(solution)/shard_map/ppermute | solution.py:16
  1354.2 366.0 %reduce-scatter.27.cloned.1.call-start = ((), (), s32[]{:S(2)}) async-start(), calls=%async_computation.14 | async-start | bytes 3981312 | tf_op jit(solution)/shard_map/reduce_scatter | solution.py:307
  1599.4 160.8 %reduce-scatter.33.cloned.1.call-start = ((), (), s32[]{:S(2)}) async-start(), calls=%async_computation.17 | async-start | bytes 1327104 | tf_op jit(solution)/shard_map/reduce_scatter | solution.py:313
  1602.0 198.0 %reduce-scatter.31.cloned.1.call-start = ((), (), s32[]{:S(2)}) async-start(), calls=%async_computation.16 | async-start | bytes 1327104 | tf_op jit(solution)/shard_map/reduce_scatter | solution.py:313
  1604.6 252.6 %reduce-scatter.37.cloned.1.call-start = ((), (), s32[]{:S(2)}) async-start(), calls=%async_computation.19 | async-start | bytes 5308416 | tf_op jit(solution)/shard_map/reduce_scatter | solution.py:316
  1609.9 304.5 %reduce-scatter.41.cloned.1.call-start = ((), (), s32[]{:S(2)}) async-start(), calls=%async_computation.21 | async-start | bytes 5308416 | tf_op jit(solution)/shard_map/reduce_scatter | solution.py:322
  1616.0 355.5 %reduce-scatter.39.cloned.1.call-start = ((), (), s32[]{:S(2)}) async-start(), calls=%async_computation.20 | async-start | bytes 5308416 | tf_op jit(solution)/shard_map/reduce_scatter | solution.py:322
  1622.2 406.4 %reduce-scatter.35.cloned.1.call-start = ((), (), s32[]{:S(2)}) async-start(), calls=%async_computation.18 | async-start | bytes 5308416 | tf_op jit(solution)/shard_map/reduce_scatter | solution.py:316
  1628.0 437.1 %reduce-scatter.53.cloned.1.call-start = ((), (), s32[]{:S(2)}) async-start(), calls=%async_computation.37 | async-start | bytes 221184
  1630.9 471.3 %reduce-scatter.49.cloned.1.call-start = ((), (), s32[]{:S(2)}) async-start(), calls=%async_computation.35 | async-start | bytes 221184
  1631.9 507.6 %reduce-scatter.45.cloned.1.call-start = ((), (), s32[]{:S(2)}) async-start(), calls=%async_computation.33 | async-start | bytes 221184
  1633.0 543.1 %reduce-scatter.51.cloned.1.call-start = ((), (), s32[]{:S(2)}) async-start(), calls=%async_computation.36 | async-start | bytes 221184
  1638.6 574.2 %reduce-scatter.47.cloned.1.call-start = ((), (), s32[]{:S(2)}) async-start(), calls=%async_computation.34 | async-start | bytes 221184
  1639.5 610.5 %reduce-scatter.43.cloned.1.call-start = ((), (), s32[]{:S(2)}) async-start(), calls=%async_computation.32 | async-start | bytes 221184
  1640.5 651.5 %all-gather.49.cloned.1.call-start = ((), (), s32[]{:S(2)}) async-start(), calls=%async_computation.31 | async-start | bytes 2211840 | tf_op jit(solution)/shard_map/all_gather | solution.py:336
  1641.2 691.3 %all-gather.47.cloned.1.call-start = ((), (), s32[]{:S(2)}) async-start(), calls=%async_computation.30 | async-start | bytes 2211840 | tf_op jit(solution)/shard_map/all_gather | solution.py:336
  1720.2 719.3 %all-reduce.11.cloned.1.call-start = ((), (), s32[]{:S(2)}) async-start(), calls=%async_computation.38 | async-start | bytes 5308416 | tf_op jit(solution)/shard_map/psum | solution.py:340
  (196 other events, 12730.2 us)
Sparse Core Ops, SparseCore 0:
  10.5 38.1 all-gather.30
  50.5 24.4 all-gather.32
  77.5 40.8 all-gather.34
  120.7 38.9 all-gather.36
  162.0 33.7 all-gather.38
  197.6 56.5 all-gather.40
  256.6 47.5 all-gather.42
  529.5 74.4 all-gather.44
  1354.3 99.2 reduce-scatter.28
  1599.4 120.7 reduce-scatter.26
  1723.4 36.6 reduce-scatter.32
  1763.3 36.6 reduce-scatter.30
  1803.4 53.7 reduce-scatter.36
  1860.5 53.7 reduce-scatter.40
  1917.6 53.7 reduce-scatter.38
  1974.7 53.7 reduce-scatter.34
  2031.4 33.6 reduce-scatter.52
  2068.6 33.6 reduce-scatter.48
  2105.9 33.6 reduce-scatter.44
  2142.4 33.6 reduce-scatter.50
  2179.1 33.6 reduce-scatter.46
  2216.4 33.6 reduce-scatter.42
  2251.6 40.2 all-gather.48
  2293.4 39.0 all-gather.46
  2335.3 104.1 all-reduce.10
